TPU v7x, 256 devices: a whole 4x4x8 slice. The times are simulated.
256 devices in a mesh: dp: 32 (over y, z), tensor: 8 (over x, core).
Axes of the slice: x: 4, y: 4, z: 8, core: 2. Of those that a mesh axis runs over, the one named last changes fastest.
Arguments:
- queries: bfloat16 [256, 6, 8192], P('dp', None, 'tensor'), may hold values from -150 to 150
- new_keys: bfloat16 [256, 6, 1024], P('dp', None, 'tensor'), may hold values from -6 to 6
- new_values: bfloat16 [256, 6, 1024], P('dp', None, 'tensor'), may hold values from -6 to 6
- key_cache: bfloat16 [256, 256, 1024], P('dp', None, 'tensor'), may hold values from -6 to 6
- value_cache: bfloat16 [256, 256, 1024], P('dp', None, 'tensor'), may hold values from -6 to 6
- cache_lengths: int32 [256], P('dp'), may hold values from 32 to 256, as said below
- accepted: int32 [256], P('tensor'), may hold values from 1 to 6
- residual: bfloat16 [256, 6, 8192], P('tensor', None, 'dp'), may hold values from -6 to 6
- out_weight: bfloat16 [8192, 8192], P('tensor', 'dp'), may hold values from -0.0625 to 0.0625
- draft_weight: bfloat16 [8192, 8192], P('tensor', 'dp'), may hold values from -0.0625 to 0.0625
Outputs:
- verified: bfloat16 [256, 6, 8192], P('tensor', None, 'dp')
- drafted: bfloat16 [5, 256, 8192], P(None, 'tensor', 'dp')
Inputs may be any that keep to these rules, and one draw needn't show every extreme that they name: `cache_lengths`: every draw has a window with all 256 slots live.
All inputs are finite; a program needn't handle non-finite values.
Results may differ from a plain program's by a relative error of at most 0.008.
Values may be sent and summed in bfloat16 or wider, within the bound.
No kernel may reach another device: no remote copies, remote signals or barrier semaphores. Data moves between devices by JAX's collectives and lax.ppermute only.
A program may use at most 64 MiB of HBM per device.

v0:
```python
import jax
import jax.numpy as jnp
from jax import lax
from jax.sharding import PartitionSpec as P

HD = 128
STEPS = 5


def widen(drafted_rows):
    wide_rows = lax.all_gather(drafted_rows, "dp", axis=1, tiled=True)
    return lax.all_to_all(wide_rows, "tensor", split_axis=1, concat_axis=0, tiled=True)


def per_device(
    queries,
    new_keys,
    new_values,
    key_cache,
    value_cache,
    cache_lengths,
    accepted,
    residual,
    out_weight,
    draft_weight,
):
    windows_here, tokens_here, query_width = queries.shape
    cache_size = key_cache.shape[1]
    kv_here = new_keys.shape[2] // HD
    group_size = query_width // HD // kv_here
    query_split = queries.reshape(windows_here, tokens_here, kv_here, group_size, HD)
    keys_cached = key_cache.reshape(windows_here, cache_size, kv_here, HD)
    keys_fresh = new_keys.reshape(windows_here, tokens_here, kv_here, HD)
    score_cache = jnp.einsum(
        "wtkgd,wpkd->wkgtp", query_split, keys_cached, preferred_element_type=jnp.float32
    ) * HD ** (-0.5)
    score_fresh = jnp.einsum(
        "wtkgd,wpkd->wkgtp", query_split, keys_fresh, preferred_element_type=jnp.float32
    ) * HD ** (-0.5)
    live_cache = (jnp.arange(cache_size)[None, :] < cache_lengths[:, None])[:, None, None, None, :]
    live_fresh = jnp.arange(tokens_here)[None, :] <= jnp.arange(tokens_here)[:, None]
    scores = jnp.concatenate(
        [
            jnp.where(live_cache, score_cache, -jnp.inf),
            jnp.where(live_fresh, score_fresh, -jnp.inf),
        ],
        axis=-1,
    )
    largest = jnp.max(scores, axis=-1, keepdims=True)
    powered = jnp.exp(scores - largest)
    weights = (powered / jnp.sum(powered, axis=-1, keepdims=True)).astype(jnp.bfloat16)
    values_cached = value_cache.reshape(windows_here, cache_size, kv_here, HD)
    values_fresh = new_values.reshape(windows_here, tokens_here, kv_here, HD)
    mixed_rows = jnp.einsum(
        "wkgtp,wpkd->wtkgd",
        weights[..., :cache_size],
        values_cached,
        preferred_element_type=jnp.float32,
    )
    mixed_rows = mixed_rows + jnp.einsum(
        "wkgtp,wpkd->wtkgd",
        weights[..., cache_size:],
        values_fresh,
        preferred_element_type=jnp.float32,
    )
    attended = mixed_rows.astype(jnp.bfloat16).reshape(windows_here * tokens_here, query_width)
    partial_out = jnp.dot(
        lax.all_gather(attended, "dp", axis=0, tiled=True),
        out_weight,
        preferred_element_type=jnp.float32,
    )
    summed = lax.psum_scatter(partial_out, "tensor", scatter_dimension=0, tiled=True)
    block_windows, block_tokens, block_cols = residual.shape
    flat_residual = residual.reshape(block_windows * block_tokens, block_cols).astype(jnp.float32)
    verified = (
        (flat_residual + summed)
        .astype(jnp.bfloat16)
        .reshape(block_windows, block_tokens, block_cols)
    )
    chosen = jnp.arange(block_tokens)[None, :] == (accepted - 1)[:, None]
    picked = jnp.sum(
        jnp.where(chosen[:, :, None], verified, jnp.zeros((), jnp.bfloat16)),
        axis=1,
        dtype=jnp.bfloat16,
    )
    results = []
    current = widen(picked)
    row_block = current.shape[0] // lax.axis_size("tensor")
    row_start = lax.axis_index("tensor") * row_block
    for draft_step in range(STEPS):
        everyone = lax.psum(
            jnp.dot(current, draft_weight, preferred_element_type=jnp.float32), "tensor"
        )
        share = lax.dynamic_slice_in_dim(everyone, row_start, row_block, 0)
        drafted_now = jnp.tanh(2.0 * share).astype(jnp.bfloat16)
        results.append(drafted_now)
        if draft_step + 1 < STEPS:
            current = widen(drafted_now)
    return (verified, jnp.stack(results))


def solution(mesh):
    placed = (
        P("dp", None, "tensor"),
        P("dp", None, "tensor"),
        P("dp", None, "tensor"),
        P("dp", None, "tensor"),
        P("dp", None, "tensor"),
        P("dp"),
        P("tensor"),
        P("tensor", None, "dp"),
        P("tensor", "dp"),
        P("tensor", "dp"),
    )
    return jax.shard_map(
        per_device,
        mesh=mesh,
        in_specs=placed,
        out_specs=(P("tensor", None, "dp"), P(None, "tensor", "dp")),
        check_vma=False,
    )
```

profile of v0, /device:TPU:8, one launch (start us, length us, event | category | flops | bytes accessed | tf_op | source)
XLA Modules:
  0.0 744.6 jit_solution(10365520250779408295)
XLA Ops:
  7.2 0.8 iota_compare_fusion.1
  8.1 1.4 fusion.17
  9.5 1.2 fusion.18
  11.1 0.9 fusion.10
  13.0 81.7 %all-gather.2.cloned.1.call-done = bf16[1536,1024]{1,0:T(8,128)(2,1)} async-done(((bf16[48,1024]{1,0:T(8,128)(2,1)}), bf16[1536,1024]{1,0:T(8,128)(2,1)}) %all-gather.2.cloned.1.call-update) | async-done | bytes 3145744 | tf_op jit(solution)/shard_map/all_gather | solution.py:68
  94.7 4.0 fusion.19
  99.0 32.9 %reduce-scatter.2.cloned.1.call-done = f32[192,256]{1,0:T(8,128)} async-done(((f32[1536,256]{1,0:T(8,128)}), f32[192,256]{1,0:T(8,128)}) %reduce-scatter.2.cloned.1.call-update) | async-done | bytes 196624 | tf_op jit(solution)/shard_map/reduce_scatter | solution.py:72
  131.9 0.9 add_convert_fusion
  133.0 43.9 %all_gather.19 = bf16[32,8192]{1,0:T(8,128)(2,1)S(1)} all-gather(bf16[32,256]{1,0:T(8,128)(2,1)S(1)} %select_reduce_fusion), channel_id=1, replica_groups=mesh['dp'=32,'tensor'=8] {'dp'}, dimensions={1}, use_global_device_ids=true | all-gather | bytes 540672 | tf_op jit(solution)/shard_map/all_gather | solution.py:11
  177.0 12.8 %all_to_all.95 = bf16[32,8,1024]{2,0,1:T(8,128)(2,1)S(1)} all-to-all(bf16[32,8,1024]{2,0,1:T(8,128)(2,1)S(1)} %bitcast.106), channel_id=1, replica_groups=mesh['dp'=32,'tensor'=8] {'tensor'}, dimensions={1} | all-to-all | bytes 1048576 | tf_op jit(solution)/shard_map/all_to_all | solution.py:12
  189.8 1.0 fusion.20
  190.9 62.3 %all-reduce.6.cloned.1.call-done = f32[256,256]{1,0:T(8,128)} async-done(((f32[256,256]{1,0:T(8,128)}), f32[256,256]{1,0:T(8,128)}) %all-reduce.6.cloned.1.call-update) | async-done | bytes 262160 | tf_op jit(solution)/shard_map/psum | solution.py:91
  253.1 0.8 bitcast_dynamic-update-slice_fusion.3
  253.9 43.9 %all_gather.20 = bf16[32,8192]{1,0:T(8,128)(2,1)S(1)} all-gather(bf16[32,256]{1,0:T(8,128)(2,1)S(1)} %get-tuple-element.17), channel_id=1, replica_groups=mesh['dp'=32,'tensor'=8] {'dp'}, dimensions={1}, use_global_device_ids=true | all-gather | bytes 540672 | tf_op jit(solution)/shard_map/all_gather | solution.py:11
  297.8 12.8 %all_to_all.96 = bf16[32,8,1024]{2,0,1:T(8,128)(2,1)S(1)} all-to-all(bf16[32,8,1024]{2,0,1:T(8,128)(2,1)S(1)} %bitcast.109), channel_id=1, replica_groups=mesh['dp'=32,'tensor'=8] {'tensor'}, dimensions={1} | all-to-all | bytes 1048576 | tf_op jit(solution)/shard_map/all_to_all | solution.py:12
  310.7 1.0 fusion.21
  311.7 62.2 %all-reduce.8.cloned.1.call-done = f32[256,256]{1,0:T(8,128)} async-done(((f32[256,256]{1,0:T(8,128)}), f32[256,256]{1,0:T(8,128)}) %all-reduce.8.cloned.1.call-update) | async-done | bytes 262160 | tf_op jit(solution)/shard_map/psum | solution.py:91
  373.9 0.8 bitcast_dynamic-update-slice_fusion.2
  374.7 43.9 %all_gather.21 = bf16[32,8192]{1,0:T(8,128)(2,1)S(1)} all-gather(bf16[32,256]{1,0:T(8,128)(2,1)S(1)} %get-tuple-element.15), channel_id=1, replica_groups=mesh['dp'=32,'tensor'=8] {'dp'}, dimensions={1}, use_global_device_ids=true | all-gather | bytes 540672 | tf_op jit(solution)/shard_map/all_gather | solution.py:11
  418.6 12.8 %all_to_all.97 = bf16[32,8,1024]{2,0,1:T(8,128)(2,1)S(1)} all-to-all(bf16[32,8,1024]{2,0,1:T(8,128)(2,1)S(1)} %bitcast.112), channel_id=1, replica_groups=mesh['dp'=32,'tensor'=8] {'tensor'}, dimensions={1} | all-to-all | bytes 1048576 | tf_op jit(solution)/shard_map/all_to_all | solution.py:12
  431.5 1.0 fusion.22
  432.5 62.2 %all-reduce.10.cloned.1.call-done = f32[256,256]{1,0:T(8,128)} async-done(((f32[256,256]{1,0:T(8,128)}), f32[256,256]{1,0:T(8,128)}) %all-reduce.10.cloned.1.call-update) | async-done | bytes 262160 | tf_op jit(solution)/shard_map/psum | solution.py:91
  494.7 0.8 bitcast_dynamic-update-slice_fusion.1
  495.5 43.9 %all_gather.22 = bf16[32,8192]{1,0:T(8,128)(2,1)S(1)} all-gather(bf16[32,256]{1,0:T(8,128)(2,1)S(1)} %get-tuple-element.13), channel_id=1, replica_groups=mesh['dp'=32,'tensor'=8] {'dp'}, dimensions={1}, use_global_device_ids=true | all-gather | bytes 540672 | tf_op jit(solution)/shard_map/all_gather | solution.py:11
  539.5 12.8 %all_to_all.98 = bf16[32,8,1024]{2,0,1:T(8,128)(2,1)S(1)} all-to-all(bf16[32,8,1024]{2,0,1:T(8,128)(2,1)S(1)} %bitcast.115), channel_id=1, replica_groups=mesh['dp'=32,'tensor'=8] {'tensor'}, dimensions={1} | all-to-all | bytes 1048576 | tf_op jit(solution)/shard_map/all_to_all | solution.py:12
  552.3 1.0 fusion.23
  553.3 62.2 %all-reduce.12.cloned.1.call-done = f32[256,256]{1,0:T(8,128)} async-done(((f32[256,256]{1,0:T(8,128)}), f32[256,256]{1,0:T(8,128)}) %all-reduce.12.cloned.1.call-update) | async-done | bytes 262160 | tf_op jit(solution)/shard_map/psum | solution.py:91
  615.5 0.8 bitcast_dynamic-update-slice_fusion
  616.3 43.9 %all_gather.23 = bf16[32,8192]{1,0:T(8,128)(2,1)S(1)} all-gather(bf16[32,256]{1,0:T(8,128)(2,1)S(1)} %get-tuple-element.11), channel_id=1, replica_groups=mesh['dp'=32,'tensor'=8] {'dp'}, dimensions={1}, use_global_device_ids=true | all-gather | bytes 540672 | tf_op jit(solution)/shard_map/all_gather | solution.py:11
  660.3 12.8 %all_to_all.99 = bf16[32,8,1024]{2,0,1:T(8,128)(2,1)S(1)} all-to-all(bf16[32,8,1024]{2,0,1:T(8,128)(2,1)S(1)} %bitcast.118), channel_id=1, replica_groups=mesh['dp'=32,'tensor'=8] {'tensor'}, dimensions={1} | all-to-all | bytes 1048576 | tf_op jit(solution)/shard_map/all_to_all | solution.py:12
  673.1 1.0 fusion.24
  674.8 61.6 %all-reduce.14.cloned.1.call-done = f32[256,256]{1,0:T(8,128)} async-done(((f32[256,256]{1,0:T(8,128)}), f32[256,256]{1,0:T(8,128)}) %all-reduce.14.cloned.1.call-update) | async-done | bytes 262160 | tf_op jit(solution)/shard_map/psum | solution.py:91
  (45 shorter events, 4.4 us)
Async XLA Ops:
  7.2 87.5 %copy-start = (bf16[1024,256]{1,0:T(8,128)(2,1)S(1)}, bf16[1024,256]{1,0:T(8,128)(2,1)}, u32[]{:S(2)}) copy-start(bf16[1024,256]{1,0:T(8,128)(2,1)} %param.18) | copy-start | bytes 1572868
  7.2 4.8 copy-start.2
  7.2 87.5 %all-gather.2.cloned.1.call-start = ((), (), s32[]{:S(2)}) async-start(), calls=%async_computation.6 | async-start | bytes 3244032 | tf_op jit(solution)/shard_map/all_gather | solution.py:68
  12.9 85.8 %copy-start.3 = (bf16[32,6,256]{2,0,1:T(8,128)(2,1)S(1)}, bf16[32,6,256]{2,0,1:T(8,128)(2,1)}, u32[]{:S(2)}) copy-start(bf16[32,6,256]{2,0,1:T(8,128)(2,1)} %param.17) | copy-start | bytes 294916
  12.9 86.0 %copy-start.5 = (s32[32]{0:T(128)S(1)}, s32[32]{0:T(128)}, u32[]{:S(2)}) copy-start(s32[32]{0:T(128)} %param.16) | copy-start | bytes 388
  12.9 118.9 %reduce-scatter.2.cloned.1.call-start = ((), (), s32[]{:S(2)}) async-start(), calls=%async_computation.7 | async-start | bytes 1769472 | tf_op jit(solution)/shard_map/reduce_scatter | solution.py:72
  98.7 91.1 %copy-start.1 = (bf16[1024,256]{1,0:T(8,128)(2,1)S(1)}, bf16[1024,256]{1,0:T(8,128)(2,1)}, u32[]{:S(2)}) copy-start(bf16[1024,256]{1,0:T(8,128)(2,1)} %param.19) | copy-start | bytes 1572868
  98.7 154.4 %all-reduce.6.cloned.1.call-start = ((), (), s32[]{:S(2)}) async-start(), calls=%async_computation.8 | async-start | bytes 524288 | tf_op jit(solution)/shard_map/psum | solution.py:91
  190.8 183.1 %all-reduce.8.cloned.1.call-start = ((), (), s32[]{:S(2)}) async-start(), calls=%async_computation.9 | async-start | bytes 524288 | tf_op jit(solution)/shard_map/psum | solution.py:91
  311.7 183.1 %all-reduce.10.cloned.1.call-start = ((), (), s32[]{:S(2)}) async-start(), calls=%async_computation.10 | async-start | bytes 524288 | tf_op jit(solution)/shard_map/psum | solution.py:91
  432.5 183.1 %all-reduce.12.cloned.1.call-start = ((), (), s32[]{:S(2)}) async-start(), calls=%async_computation.11 | async-start | bytes 524288 | tf_op jit(solution)/shard_map/psum | solution.py:91
  553.3 183.1 %all-reduce.14.cloned.1.call-start = ((), (), s32[]{:S(2)}) async-start(), calls=%async_computation.12 | async-start | bytes 524288 | tf_op jit(solution)/shard_map/psum | solution.py:91
  737.1 0.6 copy-start.4
Sparse Core Ops, SparseCore 0:
  13.0 81.5 all-gather.1
  98.8 32.9 reduce-scatter.1
  190.9 62.1 all-reduce.5
  311.8 62.0 all-reduce.7
  432.6 62.1 all-reduce.9
  553.4 62.0 all-reduce.11
  674.2 62.1 all-reduce.13
where the time goes:
time: 745 us
  waiting for transfers between devices  425 us (57%)
  blocking collectives  284 us (38%)
  between operations  14.3 us (2%)
  matrix products  12.6 us (2%)
    psum x5, waiting for transfers between devices, per_device(): lax.psum(jnp.dot(current, draft_weight, preferred_element_type=jnp.float3...  311 us
    all_gather x5, blocking collectives, widen(): wide_rows = lax.all_gather(drafted_rows, 'dp', axis=1, tiled=True)  220 us
    all_gather x1, waiting for transfers between devices, per_device(): lax.all_gather(attended, 'dp', axis=0, tiled=True)  81.7 us
    all_to_all x5, blocking collectives, widen(): lax.all_to_all(wide_rows, 'tensor', split_axis=1, concat_axis=0, tiled=True)  64 us
    reduce_scatter x1, waiting for transfers between devices, per_device(): lax.psum_scatter(partial_out, 'tensor', scatter_dimension=0, tiled=True)  32.9 us
  transfers between devices with their start and end apart: 7, of which 7 were waited for; matrix products, arithmetic and copies ran while one was open for 0% of the time, Pallas kernels for 0%

commit v1 on v0

--- a/solution.py
+++ b/solution.py
@@ -88,8 +88,11 @@
     row_block = current.shape[0] // lax.axis_size("tensor")
     row_start = lax.axis_index("tensor") * row_block
     for draft_step in range(STEPS):
-        everyone = lax.psum(
-            jnp.dot(current, draft_weight, preferred_element_type=jnp.float32), "tensor"
+        everyone = jnp.sum(
+            lax.all_gather(
+                jnp.dot(current, draft_weight, preferred_element_type=jnp.float32), "tensor"
+            ),
+            axis=0,
         )
         share = lax.dynamic_slice_in_dim(everyone, row_start, row_block, 0)
         drafted_now = jnp.tanh(2.0 * share).astype(jnp.bfloat16)

time: 745 us -> 569 us (0.76)
  waiting for transfers between devices: 425 us -> 239 us
    psum x5 -> x0, waiting for transfers between devices: 311 us -> none  [per_device(): lax.psum(jnp.dot(current, draft_weight, preferred_element_type=jnp.float3...]
    all_gather x0 -> x5, waiting for transfers between devices: none -> 124 us  [per_device(): lax.all_gather(jnp.dot(current, draft_weight, preferred_element_type=jnp....]
    reduce_sum x0 -> x5, other arithmetic: none -> 8.77 us  [per_device(): jnp.sum(lax.all_gather(jnp.dot(current, draft_weight, preferred_element_t...]
where the time goes in v1:
time: 569 us; the launch traced here: 567 us
  blocking collectives  287 us (50%)
  waiting for transfers between devices  239 us (42%)
  between operations  14.4 us (3%)
  matrix products  12 us (2%)
  other arithmetic  11.3 us (2%)
    all_gather x5, blocking collectives, widen(): wide_rows = lax.all_gather(drafted_rows, 'dp', axis=1, tiled=True)  221 us
    all_gather x5, waiting for transfers between devices, per_device(): lax.all_gather(jnp.dot(current, draft_weight, preferred_element_type=jnp....  124 us
    all_gather x1, waiting for transfers between devices, per_device(): lax.all_gather(attended, 'dp', axis=0, tiled=True)  81.7 us
    all_to_all x5, blocking collectives, widen(): lax.all_to_all(wide_rows, 'tensor', split_axis=1, concat_axis=0, tiled=True)  66.7 us
    reduce_scatter x1, waiting for transfers between devices, per_device(): lax.psum_scatter(partial_out, 'tensor', scatter_dimension=0, tiled=True)  32.5 us
  transfers between devices with their start and end apart: 7, of which 7 were waited for; matrix products, arithmetic and copies ran while one was open for 0% of the time, Pallas kernels for 0%

profile of v1, /device:TPU:8, one launch (start us, length us, event | category | flops | bytes accessed | tf_op | source)
XLA Modules:
  0.0 566.7 jit_solution(7671966744528057891)
XLA Ops:
  7.3 0.8 iota_compare_fusion.1
  8.1 1.4 fusion.17
  9.5 1.2 fusion.18
  12.3 81.7 %all-gather.12.cloned.1.call-done = bf16[1536,1024]{1,0:T(8,128)(2,1)} async-done(((bf16[48,1024]{1,0:T(8,128)(2,1)}), bf16[1536,1024]{1,0:T(8,128)(2,1)}) %all-gather.12.cloned.1.call-update) | async-done | bytes 3145744 | tf_op jit(solution)/shard_map/all_gather | solution.py:68
  94.0 4.0 fusion.19
  98.7 32.5 %reduce-scatter.2.cloned.1.call-done = f32[192,256]{1,0:T(8,128)} async-done(((f32[1536,256]{1,0:T(8,128)}), f32[192,256]{1,0:T(8,128)}) %reduce-scatter.2.cloned.1.call-update) | async-done | bytes 196624 | tf_op jit(solution)/shard_map/reduce_scatter | solution.py:72
  131.3 0.9 add_convert_fusion
  132.4 43.8 %all_gather.49 = bf16[32,8192]{1,0:T(8,128)(2,1)S(1)} all-gather(bf16[32,256]{1,0:T(8,128)(2,1)S(1)} %select_reduce_fusion), channel_id=1, replica_groups=mesh['dp'=32,'tensor'=8] {'dp'}, dimensions={1}, use_global_device_ids=true | all-gather | bytes 540672 | tf_op jit(solution)/shard_map/all_gather | solution.py:11
  176.3 12.8 %all_to_all.95 = bf16[32,8,1024]{2,0,1:T(8,128)(2,1)S(1)} all-to-all(bf16[32,8,1024]{2,0,1:T(8,128)(2,1)S(1)} %bitcast.116), channel_id=1, replica_groups=mesh['dp'=32,'tensor'=8] {'tensor'}, dimensions={1} | all-to-all | bytes 1048576 | tf_op jit(solution)/shard_map/all_to_all | solution.py:12
  189.1 1.0 fusion.20
  190.2 25.1 %all-gather.14.cloned.1.call-done = f32[2048,256]{1,0:T(8,128)} async-done(((f32[256,256]{1,0:T(8,128)}), f32[2048,256]{1,0:T(8,128)}) %all-gather.14.cloned.1.call-update) | async-done | bytes 2097168 | tf_op jit(solution)/shard_map/all_gather | solution.py:92
  215.3 1.8 reduce_sum.65
  217.1 44.2 %all_gather.52 = bf16[32,8192]{1,0:T(8,128)(2,1)S(1)} all-gather(bf16[32,256]{1,0:T(8,128)(2,1)S(1)} %get-tuple-element.17), channel_id=1, replica_groups=mesh['dp'=32,'tensor'=8] {'dp'}, dimensions={1}, use_global_device_ids=true | all-gather | bytes 540672 | tf_op jit(solution)/shard_map/all_gather | solution.py:11
  261.3 13.5 %all_to_all.96 = bf16[32,8,1024]{2,0,1:T(8,128)(2,1)S(1)} all-to-all(bf16[32,8,1024]{2,0,1:T(8,128)(2,1)S(1)} %bitcast.119), channel_id=1, replica_groups=mesh['dp'=32,'tensor'=8] {'tensor'}, dimensions={1} | all-to-all | bytes 1048576 | tf_op jit(solution)/shard_map/all_to_all | solution.py:12
  274.8 1.0 fusion.21
  275.8 25.0 %all-gather.16.cloned.1.call-done = f32[2048,256]{1,0:T(8,128)} async-done(((f32[256,256]{1,0:T(8,128)}), f32[2048,256]{1,0:T(8,128)}) %all-gather.16.cloned.1.call-update) | async-done | bytes 2097168 | tf_op jit(solution)/shard_map/all_gather | solution.py:92
  300.8 1.8 reduce_sum.66
  302.6 44.2 %all_gather.55 = bf16[32,8192]{1,0:T(8,128)(2,1)S(1)} all-gather(bf16[32,256]{1,0:T(8,128)(2,1)S(1)} %get-tuple-element.15), channel_id=1, replica_groups=mesh['dp'=32,'tensor'=8] {'dp'}, dimensions={1}, use_global_device_ids=true | all-gather | bytes 540672 | tf_op jit(solution)/shard_map/all_gather | solution.py:11
  346.8 13.5 %all_to_all.97 = bf16[32,8,1024]{2,0,1:T(8,128)(2,1)S(1)} all-to-all(bf16[32,8,1024]{2,0,1:T(8,128)(2,1)S(1)} %bitcast.122), channel_id=1, replica_groups=mesh['dp'=32,'tensor'=8] {'tensor'}, dimensions={1} | all-to-all | bytes 1048576 | tf_op jit(solution)/shard_map/all_to_all | solution.py:12
  360.3 1.0 fusion.22
  361.4 25.0 %all-gather.18.cloned.1.call-done = f32[2048,256]{1,0:T(8,128)} async-done(((f32[256,256]{1,0:T(8,128)}), f32[2048,256]{1,0:T(8,128)}) %all-gather.18.cloned.1.call-update) | async-done | bytes 2097168 | tf_op jit(solution)/shard_map/all_gather | solution.py:92
  386.4 1.8 reduce_sum.67
  388.1 44.2 %all_gather.58 = bf16[32,8192]{1,0:T(8,128)(2,1)S(1)} all-gather(bf16[32,256]{1,0:T(8,128)(2,1)S(1)} %get-tuple-element.13), channel_id=1, replica_groups=mesh['dp'=32,'tensor'=8] {'dp'}, dimensions={1}, use_global_device_ids=true | all-gather | bytes 540672 | tf_op jit(solution)/shard_map/all_gather | solution.py:11
  432.4 13.5 %all_to_all.98 = bf16[32,8,1024]{2,0,1:T(8,128)(2,1)S(1)} all-to-all(bf16[32,8,1024]{2,0,1:T(8,128)(2,1)S(1)} %bitcast.125), channel_id=1, replica_groups=mesh['dp'=32,'tensor'=8] {'tensor'}, dimensions={1} | all-to-all | bytes 1048576 | tf_op jit(solution)/shard_map/all_to_all | solution.py:12
  445.8 1.0 fusion.23
  446.9 25.0 %all-gather.20.cloned.1.call-done = f32[2048,256]{1,0:T(8,128)} async-done(((f32[256,256]{1,0:T(8,128)}), f32[2048,256]{1,0:T(8,128)}) %all-gather.20.cloned.1.call-update) | async-done | bytes 2097168 | tf_op jit(solution)/shard_map/all_gather | solution.py:92
  471.9 1.8 reduce_sum.68
  473.7 44.2 %all_gather.61 = bf16[32,8192]{1,0:T(8,128)(2,1)S(1)} all-gather(bf16[32,256]{1,0:T(8,128)(2,1)S(1)} %get-tuple-element.11), channel_id=1, replica_groups=mesh['dp'=32,'tensor'=8] {'dp'}, dimensions={1}, use_global_device_ids=true | all-gather | bytes 540672 | tf_op jit(solution)/shard_map/all_gather | solution.py:11
  517.9 13.5 %all_to_all.99 = bf16[32,8,1024]{2,0,1:T(8,128)(2,1)S(1)} all-to-all(bf16[32,8,1024]{2,0,1:T(8,128)(2,1)S(1)} %bitcast.128), channel_id=1, replica_groups=mesh['dp'=32,'tensor'=8] {'tensor'}, dimensions={1} | all-to-all | bytes 1048576 | tf_op jit(solution)/shard_map/all_to_all | solution.py:12
  531.4 1.0 fusion.24
  533.1 24.4 %all-gather.22.cloned.1.call-done = f32[2048,256]{1,0:T(8,128)} async-done(((f32[256,256]{1,0:T(8,128)}), f32[2048,256]{1,0:T(8,128)}) %all-gather.22.cloned.1.call-update) | async-done | bytes 2097168 | tf_op jit(solution)/shard_map/all_gather | solution.py:92
  557.4 1.8 reduce_sum.69
  (52 shorter events, 4.3 us)
Async XLA Ops:
  7.2 86.8 %copy-start = (bf16[1024,256]{1,0:T(8,128)(2,1)S(1)}, bf16[1024,256]{1,0:T(8,128)(2,1)}, u32[]{:S(2)}) copy-start(bf16[1024,256]{1,0:T(8,128)(2,1)} %param.18) | copy-start | bytes 1572868
  7.2 4.0 copy-start.4
  7.2 4.1 copy-start.2
  7.2 86.8 %all-gather.12.cloned.1.call-start = ((), (), s32[]{:S(2)}) async-start(), calls=%async_computation.6 | async-start | bytes 3244032 | tf_op jit(solution)/shard_map/all_gather | solution.py:68
  12.2 85.9 %copy-start.3 = (bf16[32,6,256]{2,0,1:T(8,128)(2,1)S(1)}, bf16[32,6,256]{2,0,1:T(8,128)(2,1)}, u32[]{:S(2)}) copy-start(bf16[32,6,256]{2,0,1:T(8,128)(2,1)} %param.17) | copy-start | bytes 294916
  12.2 119.0 %reduce-scatter.2.cloned.1.call-start = ((), (), s32[]{:S(2)}) async-start(), calls=%async_computation.7 | async-start | bytes 1769472 | tf_op jit(solution)/shard_map/reduce_scatter | solution.py:72
  98.0 0.7 copy-start.6
  98.0 91.1 %copy-start.1 = (bf16[1024,256]{1,0:T(8,128)(2,1)S(1)}, bf16[1024,256]{1,0:T(8,128)(2,1)}, u32[]{:S(2)}) copy-start(bf16[1024,256]{1,0:T(8,128)(2,1)} %param.19) | copy-start | bytes 1572868
  98.0 117.3 %all-gather.14.cloned.1.call-start = ((), (), s32[]{:S(2)}) async-start(), calls=%async_computation.8 | async-start | bytes 2359296 | tf_op jit(solution)/shard_map/all_gather | solution.py:92
  190.1 110.7 %all-gather.16.cloned.1.call-start = ((), (), s32[]{:S(2)}) async-start(), calls=%async_computation.9 | async-start | bytes 2359296 | tf_op jit(solution)/shard_map/all_gather | solution.py:92
  275.8 110.6 %all-gather.18.cloned.1.call-start = ((), (), s32[]{:S(2)}) async-start(), calls=%async_computation.10 | async-start | bytes 2359296 | tf_op jit(solution)/shard_map/all_gather | solution.py:92
  361.3 110.6 %all-gather.20.cloned.1.call-start = ((), (), s32[]{:S(2)}) async-start(), calls=%async_computation.11 | async-start | bytes 2359296 | tf_op jit(solution)/shard_map/all_gather | solution.py:92
  446.9 110.6 %all-gather.22.cloned.1.call-start = ((), (), s32[]{:S(2)}) async-start(), calls=%async_computation.12 | async-start | bytes 2359296 | tf_op jit(solution)/shard_map/all_gather | solution.py:92
  559.2 0.6 copy-start.5
Sparse Core Ops, SparseCore 0:
  12.3 81.5 all-gather.11
  98.1 33.0 reduce-scatter.1
  190.2 24.9 all-gather.13
  275.9 24.8 all-gather.15
  361.5 24.8 all-gather.17
  447.0 24.8 all-gather.19
  532.5 24.8 all-gather.21
